TPU v7x, 256 devices: a whole 4x4x8 slice. The times are simulated.
256 devices in a mesh: grp: 8 (over y, core), sub: 32 (over x, z).
Axes of the slice: x: 4, y: 4, z: 8, core: 2. Of those that a mesh axis runs over, the one named last changes fastest.
Arguments:
- cluster_pos: float32 [3, 4096], P(None, 'sub'), may hold values from -3 to 3
- cluster_vel: float32 [3, 4096], P(None, 'sub'), may hold values from -15 to 15
- cluster_mass: float32 [4096], P('sub'), may hold values from 3 to 60
- galaxy_pos: float32 [3, 131072], P(None, ('grp', 'sub')), may hold values from -1 to 7
- galaxy_vel: float32 [3, 131072], P(None, ('grp', 'sub')), may hold values from -3 to 3
- galaxy_kind: int32 [131072], P(('grp', 'sub')), may hold values from 0 to 3
- species_mass: float32 [4], replicated, may hold values from 10 to 80
Outputs:
- cluster_pos_out: float32 [3, 4096], P(None, 'sub')
- cluster_vel_out: float32 [3, 4096], P(None, 'sub')
- galaxy_pos_out: float32 [3, 131072], P(None, ('grp', 'sub'))
- galaxy_vel_out: float32 [3, 131072], P(None, ('grp', 'sub'))
All inputs are finite; a program needn't handle non-finite values.
Results may differ from a plain program's by a relative error of at most 0.0003.
Values sent between devices are 32-bit elements; how exact they have to be, the bound alone decides.
A program may use at most 64 MiB of HBM per device.

v0:
```python
import jax
import jax.numpy as jnp
from jax import lax
from jax.sharding import PartitionSpec as P

SUBSTEPS = 8
step_time = 0.5
bridge_soft = 0.01
cluster_soft = 0.0025
tile_limit = 524288


def pick_block(target_count, source_count):
    tile_size = target_count
    while tile_size > 1 and (
        tile_size * source_count > tile_limit or target_count % tile_size != 0
    ):
        tile_size = tile_size // 2
    return tile_size


def field(targets, sources, masses, soften):
    target_count = targets.shape[1]
    tile_size = pick_block(target_count, sources.shape[1])

    def field_one_tile(target_tile):
        separation = sources[:, None, :] - target_tile[:, :, None]
        distance = jnp.sum(separation * separation, axis=0) + soften
        inverse = lax.rsqrt(distance)
        weight = masses[None, :] * inverse * inverse * inverse
        return jnp.sum(separation * weight[None], axis=2)

    stacked = targets.reshape(3, target_count // tile_size, tile_size).transpose(1, 0, 2)
    result = lax.map(field_one_tile, stacked)
    return result.transpose(1, 0, 2).reshape(3, target_count)


def rates(target_pos, target_vel, source_pos, source_vel, masses, soften):
    target_count = target_pos.shape[1]
    tile_size = pick_block(target_count, source_pos.shape[1])

    def rates_one_tile(target_tile):
        separation = source_pos[:, None, :] - target_tile[:3, :, None]
        closing = source_vel[:, None, :] - target_tile[3:, :, None]
        distance = jnp.sum(separation * separation, axis=0) + soften
        inverse = lax.rsqrt(distance)
        weight = masses[None, :] * inverse * inverse * inverse
        radial = 3.0 * jnp.sum(separation * closing, axis=0) / distance
        acceleration = jnp.sum(separation * weight[None], axis=2)
        jerk_rate = jnp.sum((closing - radial[None] * separation) * weight[None], axis=2)
        return jnp.concatenate([acceleration, jerk_rate], axis=0)

    stacked = jnp.concatenate([target_pos, target_vel], axis=0)
    stacked = stacked.reshape(6, target_count // tile_size, tile_size).transpose(1, 0, 2)
    result = lax.map(rates_one_tile, stacked)
    return result.transpose(1, 0, 2).reshape(6, target_count)


def local(
    cluster_pos, cluster_vel, cluster_mass, galaxy_pos, galaxy_vel, galaxy_kind, species_mass
):
    star_count = cluster_pos.shape[1]
    member_count = lax.axis_size("sub")
    group_count = lax.axis_size("grp")
    total_stars = star_count * member_count
    total_bodies = galaxy_pos.shape[1] * member_count * group_count
    star_mass = cluster_mass / total_stars
    species = jnp.arange(species_mass.shape[0], dtype=jnp.int32)
    body_mass = (
        jnp.sum(
            jnp.where(galaxy_kind[None, :] == species[:, None], species_mass[:, None], 0.0), axis=0
        )
        / total_bodies
    )
    half_step = step_time / 2.0

    def kick(star_positions, body_positions):
        stacked = jnp.concatenate([star_positions, star_mass[None, :]], axis=0)
        gathered = lax.all_gather(stacked, "sub", axis=1, tiled=True)
        galaxy_push = field(body_positions, gathered[:3], gathered[3], bridge_soft)
        partial_value = field(gathered[:3], body_positions, body_mass, bridge_soft)
        summed = lax.psum(partial_value, ("grp", "sub"))
        cluster_pull = lax.dynamic_slice_in_dim(
            summed, lax.axis_index("sub") * star_count, star_count, 1
        )
        return (cluster_pull, galaxy_push)

    def evaluate(guess_pos, guess_vel):
        sources = jnp.concatenate([guess_pos, guess_vel, star_mass[None, :]], axis=0)
        target_pos, target_vel = (guess_pos, guess_vel)
        source_piece = lax.all_gather(sources, "sub", axis=1, tiled=True)
        result = rates(
            target_pos,
            target_vel,
            source_piece[:3],
            source_piece[3:6],
            source_piece[6],
            cluster_soft,
        )
        return (result[:3], result[3:])

    first_pull, first_push = kick(cluster_pos, galaxy_pos)
    star_vel = cluster_vel + half_step * first_pull
    body_vel = galaxy_vel + half_step * first_push
    body_pos = galaxy_pos + step_time * body_vel
    substep_time = step_time / SUBSTEPS
    positions, velocity = (cluster_pos, star_vel)
    acceleration, jerk_rate = evaluate(positions, velocity)
    for substep in range(SUBSTEPS):
        guess_pos = positions + substep_time * (
            velocity + substep_time * (acceleration / 2.0 + substep_time * jerk_rate / 6.0)
        )
        guess_vel = velocity + substep_time * (acceleration + substep_time * jerk_rate / 2.0)
        new_acc, new_jerk = evaluate(guess_pos, guess_vel)
        new_vel = (
            velocity
            + substep_time / 2.0 * (acceleration + new_acc)
            + substep_time * substep_time / 12.0 * (jerk_rate - new_jerk)
        )
        new_pos = (
            positions
            + substep_time / 2.0 * (velocity + new_vel)
            + substep_time * substep_time / 12.0 * (acceleration - new_acc)
        )
        positions, velocity, acceleration, jerk_rate = (new_pos, new_vel, new_acc, new_jerk)
    second_pull, second_push = kick(positions, body_pos)
    return (
        positions,
        velocity + half_step * second_pull,
        body_pos,
        body_vel + half_step * second_push,
    )


def solution(mesh):
    return jax.shard_map(
        local,
        mesh=mesh,
        in_specs=(
            P(None, "sub"),
            P(None, "sub"),
            P("sub"),
            P(None, ("grp", "sub")),
            P(None, ("grp", "sub")),
            P(("grp", "sub")),
            P(),
        ),
        out_specs=(
            P(None, "sub"),
            P(None, "sub"),
            P(None, ("grp", "sub")),
            P(None, ("grp", "sub")),
        ),
        check_vma=False,
    )
```

profile of v0, /device:TPU:1, one launch (start us, length us, event | category | flops | bytes accessed | tf_op | source)
XLA Modules:
  0.0 715.4 jit_solution(4176489332510097580)
XLA Ops:
  2.0 40.5 %all_gather.33 = f32[4,4096]{1,0:T(4,128)S(1)} all-gather(f32[4,128]{1,0:T(4,128)S(1)} %pad_maximum_fusion.10), channel_id=1, replica_groups=mesh['grp'=8,'sub'=32] {'sub'}, dimensions={1}, use_global_device_ids=true | all-gather | bytes 67584 | tf_op jit(solution)/shard_map/all_gather | solution.py:79
  43.3 14.5 %while.8 = (s32[]{:T(128)}, f32[4,3,1024]{2,1,0:T(4,128)S(1)}, f32[3,512]{1,0:T(4,128)}, f32[4,3,1024]{2,1,0:T(4,128)S(1)}, f32[512]{0:T(512)S(1)}, /*index=5*/s32[]{:T(128)}) while((s32[]{:T(128)}, f32[4,3,1024]{2,1,0:T(4,128)S(1)}, f32[3,512]{1,0:T(4,128)}, f32[4,3,1024]{2,1,0:T(4,128)S(1)}, f32[512]{0:T(512)S(1)}, ...), condition=%wide.region_4.5_spmd, body=%wide.region_1.4_spmd.sunk | while | flops 11006978 | bytes 8521833 | solution.py:34
  57.8 87.6 %psum.14 = f32[3,4096]{1,0:T(4,128)S(1)} all-reduce(f32[3,4096]{1,0:T(4,128)S(1)} %bitcast.93), channel_id=1, replica_groups=mesh['grp'=8,'sub'=32] {'grp','sub'}, use_global_device_ids=true, to_apply=%region_5.6 | all-reduce | flops 12288 | bytes 98304 | tf_op jit(solution)/shard_map/psum | solution.py:82
  145.4 31.0 %all_gather.34 = f32[7,4096]{1,0:T(8,128)S(1)} all-gather(f32[7,128]{1,0:T(8,128)S(1)} %pad_maximum_fusion.8), channel_id=1, replica_groups=mesh['grp'=8,'sub'=32] {'sub'}, dimensions={1}, use_global_device_ids=true | all-gather | bytes 118272 | tf_op jit(solution)/shard_map/all_gather | solution.py:91
  179.0 2.1 fusion.27
  181.2 32.3 %all_gather.35 = f32[7,4096]{1,0:T(8,128)S(1)} all-gather(f32[7,128]{1,0:T(8,128)S(1)} %pad_maximum_fusion.7), channel_id=1, replica_groups=mesh['grp'=8,'sub'=32] {'sub'}, dimensions={1}, use_global_device_ids=true | all-gather | bytes 118272 | tf_op jit(solution)/shard_map/all_gather | solution.py:91
  213.5 2.0 fusion.31
  216.2 2.2 fusion.11
  218.4 31.8 %all_gather.36 = f32[7,4096]{1,0:T(8,128)S(1)} all-gather(f32[7,128]{1,0:T(8,128)S(1)} %pad_maximum_fusion.6), channel_id=1, replica_groups=mesh['grp'=8,'sub'=32] {'sub'}, dimensions={1}, use_global_device_ids=true | all-gather | bytes 118272 | tf_op jit(solution)/shard_map/all_gather | solution.py:91
  250.2 2.0 fusion.34
  252.9 2.2 fusion.13
  255.1 33.7 %all_gather.37 = f32[7,4096]{1,0:T(8,128)S(1)} all-gather(f32[7,128]{1,0:T(8,128)S(1)} %pad_maximum_fusion.5), channel_id=1, replica_groups=mesh['grp'=8,'sub'=32] {'sub'}, dimensions={1}, use_global_device_ids=true | all-gather | bytes 118272 | tf_op jit(solution)/shard_map/all_gather | solution.py:91
  288.9 2.0 fusion.37
  291.5 2.2 fusion.15
  293.7 30.9 %all_gather.38 = f32[7,4096]{1,0:T(8,128)S(1)} all-gather(f32[7,128]{1,0:T(8,128)S(1)} %pad_maximum_fusion.4), channel_id=1, replica_groups=mesh['grp'=8,'sub'=32] {'sub'}, dimensions={1}, use_global_device_ids=true | all-gather | bytes 118272 | tf_op jit(solution)/shard_map/all_gather | solution.py:91
  324.6 2.0 fusion.40
  327.3 2.2 fusion.17
  329.5 33.5 %all_gather.39 = f32[7,4096]{1,0:T(8,128)S(1)} all-gather(f32[7,128]{1,0:T(8,128)S(1)} %pad_maximum_fusion.3), channel_id=1, replica_groups=mesh['grp'=8,'sub'=32] {'sub'}, dimensions={1}, use_global_device_ids=true | all-gather | bytes 118272 | tf_op jit(solution)/shard_map/all_gather | solution.py:91
  363.0 2.0 fusion.43
  365.7 2.2 fusion.19
  367.9 30.7 %all_gather.40 = f32[7,4096]{1,0:T(8,128)S(1)} all-gather(f32[7,128]{1,0:T(8,128)S(1)} %pad_maximum_fusion.2), channel_id=1, replica_groups=mesh['grp'=8,'sub'=32] {'sub'}, dimensions={1}, use_global_device_ids=true | all-gather | bytes 118272 | tf_op jit(solution)/shard_map/all_gather | solution.py:91
  398.6 2.0 fusion.46
  401.3 2.2 fusion.21
  403.5 33.4 %all_gather.41 = f32[7,4096]{1,0:T(8,128)S(1)} all-gather(f32[7,128]{1,0:T(8,128)S(1)} %pad_maximum_fusion.1), channel_id=1, replica_groups=mesh['grp'=8,'sub'=32] {'sub'}, dimensions={1}, use_global_device_ids=true | all-gather | bytes 118272 | tf_op jit(solution)/shard_map/all_gather | solution.py:91
  439.6 2.2 fusion.23
  441.8 31.1 %all_gather.42 = f32[7,4096]{1,0:T(8,128)S(1)} all-gather(f32[7,128]{1,0:T(8,128)S(1)} %pad_maximum_fusion), channel_id=1, replica_groups=mesh['grp'=8,'sub'=32] {'sub'}, dimensions={1}, use_global_device_ids=true | all-gather | bytes 118272 | tf_op jit(solution)/shard_map/all_gather | solution.py:91
  475.6 2.2 fusion.25
  477.9 36.5 %all_gather.43 = f32[4,4096]{1,0:T(4,128)S(1)} all-gather(f32[4,128]{1,0:T(4,128)S(1)} %pad_maximum_fusion.9), channel_id=1, replica_groups=mesh['grp'=8,'sub'=32] {'sub'}, dimensions={1}, use_global_device_ids=true | all-gather | bytes 67584 | tf_op jit(solution)/shard_map/all_gather | solution.py:79
  514.4 8.5 %while.9 = (s32[]{:T(128)}, f32[4,3,128]{2,1,0:T(4,128)S(1)}, f32[3,4096]{1,0:T(4,128)S(1)}, f32[4,3,128]{2,1,0:T(4,128)S(1)}, f32[1,4096]{1,0:T(1,128)S(1)}, /*index=5*/s32[]{:T(128)}) while((s32[]{:T(128)}, f32[4,3,128]{2,1,0:T(4,128)S(1)}, f32[3,4096]{1,0:T(4,128)S(1)}, f32[4,3,128]{2,1,0:T(4,128)S(1)}, f32[1,4096]{1,0:T(1,128)S(1)}, ...), condition=%wide.region_45.46_spmd, body=%wide.region_42.45_spmd.sunk | while | flops 11009666 | bytes 8515149 | solution.py:34
  523.0 8.5 %while.11 = (s32[]{:T(128)}, f32[4,3,128]{2,1,0:T(4,128)S(1)}, f32[3,4096]{1,0:T(4,128)S(1)}, f32[4,3,128]{2,1,0:T(4,128)S(1)}, f32[1,4096]{1,0:T(1,128)S(1)}, /*index=5*/s32[]{:T(128)}) while((s32[]{:T(128)}, f32[4,3,128]{2,1,0:T(4,128)S(1)}, f32[3,4096]{1,0:T(4,128)S(1)}, f32[4,3,128]{2,1,0:T(4,128)S(1)}, f32[1,4096]{1,0:T(1,128)S(1)}, ...), condition=%wide.region_54.55_spmd, body=%wide.region_51.54_spmd.sunk | while | flops 11009666 | bytes 8515149 | solution.py:34
  532.1 10.4 %while.10 = (s32[]{:T(128)}, f32[4,3,1024]{2,1,0:T(4,128)S(1)}, f32[3,512]{1,0:T(4,128)S(1)}, f32[4,3,1024]{2,1,0:T(4,128)S(1)}, f32[512]{0:T(512)S(1)}, /*index=5*/s32[]{:T(128)}) while((s32[]{:T(128)}, f32[4,3,1024]{2,1,0:T(4,128)S(1)}, f32[3,512]{1,0:T(4,128)S(1)}, f32[4,3,1024]{2,1,0:T(4,128)S(1)}, f32[512]{0:T(512)S(1)}, ...), condition=%wide.region_49.50_spmd, body=%wide.region_46.49_spmd.sunk | while | flops 11006978 | bytes 8497229 | solution.py:34
  542.5 171.9 %psum.15 = f32[3,4096]{1,0:T(4,128)S(1)} all-reduce(f32[3,4096]{1,0:T(4,128)S(1)} %bitcast.92), channel_id=1, replica_groups=mesh['grp'=8,'sub'=32] {'grp','sub'}, use_global_device_ids=true, to_apply=%region_50.51 | all-reduce | flops 12288 | bytes 98304 | tf_op jit(solution)/shard_map/psum | solution.py:82
  (166 shorter events, 56.3 us)
Async XLA Ops:
  43.2 102.1 %copy-start.6 = (f32[3,128]{1,0:T(4,128)S(1)}, f32[3,128]{1,0:T(4,128)}, u32[]{:S(2)}) copy-start(f32[3,128]{1,0:T(4,128)} %param.16) | copy-start | bytes 4612
  43.2 102.1 %copy-start.3 = (f32[3,128]{1,0:T(4,128)S(1)}, f32[3,128]{1,0:T(4,128)}, u32[]{:S(2)}) copy-start(f32[3,128]{1,0:T(4,128)} %param.15) | copy-start | bytes 4612
  44.9 0.7 copy-start
  48.6 0.7 copy-start
  52.2 0.7 copy-start
  55.8 0.7 copy-start
  475.6 38.8 %copy-start.1 = (f32[3,512]{1,0:T(4,128)S(1)}, f32[3,512]{1,0:T(4,128)}, u32[]{:S(2)}) copy-start(f32[3,512]{1,0:T(4,128)} %get-tuple-element.607) | copy-start | bytes 18436
  477.8 36.6 %copy-start.5 = (f32[3,128]{1,0:T(4,128)}, f32[3,128]{1,0:T(4,128)S(1)}, u32[]{:S(2)}) copy-start(f32[3,128]{1,0:T(4,128)S(1)} %multiply_add_fusion.2) | copy-start | bytes 4612
  514.4 8.5 %copy-start.4 = (f32[3,512]{1,0:T(4,128)S(1)}, f32[3,512]{1,0:T(4,128)}, u32[]{:S(2)}) copy-start(f32[3,512]{1,0:T(4,128)} %param.19) | copy-start | bytes 18436
  542.5 172.5 %copy-start.2 = (f32[3,512]{1,0:T(4,128)}, f32[3,512]{1,0:T(4,128)S(1)}, u32[]{:S(2)}) copy-start(f32[3,512]{1,0:T(4,128)S(1)} %get-tuple-element.610) | copy-start | bytes 18436
where the time goes:
time: 725 us; the launch traced here: 715 us
  blocking collectives  625 us (86%)
  other arithmetic  86 us (12%)
    all_gather x9, blocking collectives, evaluate(): source_piece = lax.all_gather(sources, 'sub', axis=1, tiled=True)  288 us
    psum x2, blocking collectives, kick(): summed = lax.psum(partial_value, ('grp', 'sub'))  259 us
    all_gather x2, blocking collectives, kick(): gathered = lax.all_gather(stacked, 'sub', axis=1, tiled=True)  76.9 us
    reduce_sum x8, other arithmetic, rates_one_tile(): jnp.sum((closing - radial[None] * separation) * weight[None], axis=2)  17.5 us
    reduce_sum x16, other arithmetic, field_one_tile(): distance = jnp.sum(separation * separation, axis=0) + soften  17.3 us
    reduce_sum x16, other arithmetic, field_one_tile(): return jnp.sum(separation * weight[None], axis=2)  16.5 us
    reduce_sum x8, other arithmetic, rates_one_tile(): radial = 3.0 * jnp.sum(separation * closing, axis=0) / distance  16.4 us

commit v1 on v0

--- a/solution.py
+++ b/solution.py
@@ -79,7 +79,8 @@
         gathered = lax.all_gather(stacked, "sub", axis=1, tiled=True)
         galaxy_push = field(body_positions, gathered[:3], gathered[3], bridge_soft)
         partial_value = field(gathered[:3], body_positions, body_mass, bridge_soft)
-        summed = lax.psum(partial_value, ("grp", "sub"))
+        shards = lax.all_gather(partial_value, ("grp", "sub"), axis=0, tiled=False)
+        summed = shards.sum(axis=0)
         cluster_pull = lax.dynamic_slice_in_dim(
             summed, lax.axis_index("sub") * star_count, star_count, 1
         )

time: 725 us -> 836 us (1.15)
  waiting for transfers between devices: 0 us -> 336 us
  blocking collectives: 625 us -> 366 us
  other arithmetic: 86 us -> 104 us
  between operations: 1.67 us -> 15.1 us
    all_gather x0 -> x2, waiting for transfers between devices: none -> 336 us  [kick(): shards = lax.all_gather(partial_value, ('grp', 'sub'), axis=0, tiled=False)]
    psum x2 -> x0, blocking collectives: 259 us -> none  [kick(): summed = lax.psum(partial_value, ('grp', 'sub'))]
    reduce_sum x0 -> x2, other arithmetic: none -> 17.6 us  [kick(): summed = shards.sum(axis=0)]
  transfers between devices with their start and end apart: 0 -> 2, of which waited for: 0 -> 2; matrix products, arithmetic and copies ran while one was open for 0% -> 3% of each run, Pallas kernels for 0% -> 0%
where the time goes in v1:
time: 836 us; the launch traced here: 829 us
  blocking collectives  366 us (44%)
  waiting for transfers between devices  336 us (40%)
  other arithmetic  104 us (12%)
  between operations  15.1 us (2%)
    all_gather x2, waiting for transfers between devices, kick(): shards = lax.all_gather(partial_value, ('grp', 'sub'), axis=0, tiled=False)  336 us
    all_gather x9, blocking collectives, evaluate(): source_piece = lax.all_gather(sources, 'sub', axis=1, tiled=True)  291 us
    all_gather x2, blocking collectives, kick(): gathered = lax.all_gather(stacked, 'sub', axis=1, tiled=True)  75.7 us
    reduce_sum x2, other arithmetic, kick(): summed = shards.sum(axis=0)  17.6 us
    reduce_sum x8, other arithmetic, rates_one_tile(): jnp.sum((closing - radial[None] * separation) * weight[None], axis=2)  17.5 us
    reduce_sum x16, other arithmetic, field_one_tile(): distance = jnp.sum(separation * separation, axis=0) + soften  17.3 us
  transfers between devices with their start and end apart: 2, of which 2 were waited for; matrix products, arithmetic and copies ran while one was open for 3% of the time, Pallas kernels for 0%

profile of v1, /device:TPU:1, one launch (start us, length us, event | category | flops | bytes accessed | tf_op | source)
XLA Modules:
  0.0 828.5 jit_solution(17297801181655927765)
XLA Ops:
  8.6 40.5 %all_gather.39 = f32[4,4096]{1,0:T(4,128)S(1)} all-gather(f32[4,128]{1,0:T(4,128)S(1)} %pad_maximum_fusion.10), channel_id=1, replica_groups=mesh['grp'=8,'sub'=32] {'sub'}, dimensions={1}, use_global_device_ids=true | all-gather | bytes 67584 | tf_op jit(solution)/shard_map/all_gather | solution.py:79
  49.8 14.5 %while.8 = (s32[]{:T(128)}, f32[4,3,1024]{2,1,0:T(4,128)S(1)}, f32[3,512]{1,0:T(4,128)}, f32[4,3,1024]{2,1,0:T(4,128)S(1)}, f32[512]{0:T(512)S(1)}, /*index=5*/s32[]{:T(128)}) while((s32[]{:T(128)}, f32[4,3,1024]{2,1,0:T(4,128)S(1)}, f32[3,512]{1,0:T(4,128)}, f32[4,3,1024]{2,1,0:T(4,128)S(1)}, f32[512]{0:T(512)S(1)}, ...), condition=%wide.region_4.5_spmd, body=%wide.region_1.4_spmd.sunk | while | flops 11006978 | bytes 8521833 | solution.py:34
  65.1 11.2 %while.9 = (s32[]{:T(128)}, f32[4,3,128]{2,1,0:T(4,128)S(1)}, f32[3,4096]{1,0:T(4,128)S(1)}, f32[4,3,128]{2,1,0:T(4,128)}, f32[1,4096]{1,0:T(1,128)S(1)}, /*index=5*/s32[]{:T(128)}) while((s32[]{:T(128)}, f32[4,3,128]{2,1,0:T(4,128)S(1)}, f32[3,4096]{1,0:T(4,128)S(1)}, f32[4,3,128]{2,1,0:T(4,128)}, f32[1,4096]{1,0:T(1,128)S(1)}, ...), condition=%wide.region_45.46_spmd, body=%wide.region_42.45_spmd.sunk | while | flops 11009666 | bytes 8515149 | solution.py:34
  77.0 124.1 %all-gather.3.cloned.1.call-done = f32[256,3,4096]{2,1,0:T(4,128)} async-done(((f32[1,3,4096]{2,1,0:T(4,128)}), f32[256,3,4096]{2,1,0:T(4,128)}) %all-gather.3.cloned.1.call-update) | async-done | bytes 12582928 | tf_op jit(solution)/shard_map/all_gather | solution.py:82
  201.0 8.8 %reduce_sum.460 = f32[3,4096]{1,0:T(4,128)S(1)} reduce(f32[256,3,4096]{2,1,0:T(4,128)} %all-gather.3.cloned.1.call-done, f32[]{:T(128)} %constant.221.clone.1), dimensions={0}, to_apply=%region_5.6 | reduce | flops 3133440 | bytes 12632068 | tf_op jit(solution)/shard_map/reduce_sum | solution.py:83
  209.9 33.2 %all_gather.41 = f32[7,4096]{1,0:T(8,128)S(1)} all-gather(f32[7,128]{1,0:T(8,128)S(1)} %pad_maximum_fusion.8), channel_id=1, replica_groups=mesh['grp'=8,'sub'=32] {'sub'}, dimensions={1}, use_global_device_ids=true | all-gather | bytes 118272 | tf_op jit(solution)/shard_map/all_gather | solution.py:92
  245.6 2.1 fusion.27
  247.8 31.9 %all_gather.42 = f32[7,4096]{1,0:T(8,128)S(1)} all-gather(f32[7,128]{1,0:T(8,128)S(1)} %pad_maximum_fusion.7), channel_id=1, replica_groups=mesh['grp'=8,'sub'=32] {'sub'}, dimensions={1}, use_global_device_ids=true | all-gather | bytes 118272 | tf_op jit(solution)/shard_map/all_gather | solution.py:92
  279.8 2.0 fusion.31
  282.4 2.2 fusion.11
  284.7 32.7 %all_gather.43 = f32[7,4096]{1,0:T(8,128)S(1)} all-gather(f32[7,128]{1,0:T(8,128)S(1)} %pad_maximum_fusion.6), channel_id=1, replica_groups=mesh['grp'=8,'sub'=32] {'sub'}, dimensions={1}, use_global_device_ids=true | all-gather | bytes 118272 | tf_op jit(solution)/shard_map/all_gather | solution.py:92
  317.4 2.0 fusion.34
  320.0 2.2 fusion.13
  322.3 32.2 %all_gather.44 = f32[7,4096]{1,0:T(8,128)S(1)} all-gather(f32[7,128]{1,0:T(8,128)S(1)} %pad_maximum_fusion.5), channel_id=1, replica_groups=mesh['grp'=8,'sub'=32] {'sub'}, dimensions={1}, use_global_device_ids=true | all-gather | bytes 118272 | tf_op jit(solution)/shard_map/all_gather | solution.py:92
  354.5 2.0 fusion.37
  357.1 2.2 fusion.15
  359.4 32.6 %all_gather.45 = f32[7,4096]{1,0:T(8,128)S(1)} all-gather(f32[7,128]{1,0:T(8,128)S(1)} %pad_maximum_fusion.4), channel_id=1, replica_groups=mesh['grp'=8,'sub'=32] {'sub'}, dimensions={1}, use_global_device_ids=true | all-gather | bytes 118272 | tf_op jit(solution)/shard_map/all_gather | solution.py:92
  392.1 2.0 fusion.40
  394.7 2.2 fusion.17
  396.9 31.6 %all_gather.46 = f32[7,4096]{1,0:T(8,128)S(1)} all-gather(f32[7,128]{1,0:T(8,128)S(1)} %pad_maximum_fusion.3), channel_id=1, replica_groups=mesh['grp'=8,'sub'=32] {'sub'}, dimensions={1}, use_global_device_ids=true | all-gather | bytes 118272 | tf_op jit(solution)/shard_map/all_gather | solution.py:92
  431.2 2.2 fusion.19
  433.4 31.9 %all_gather.47 = f32[7,4096]{1,0:T(8,128)S(1)} all-gather(f32[7,128]{1,0:T(8,128)S(1)} %pad_maximum_fusion.2), channel_id=1, replica_groups=mesh['grp'=8,'sub'=32] {'sub'}, dimensions={1}, use_global_device_ids=true | all-gather | bytes 118272 | tf_op jit(solution)/shard_map/all_gather | solution.py:92
  468.0 2.2 fusion.21
  470.2 32.1 %all_gather.48 = f32[7,4096]{1,0:T(8,128)S(1)} all-gather(f32[7,128]{1,0:T(8,128)S(1)} %pad_maximum_fusion.1), channel_id=1, replica_groups=mesh['grp'=8,'sub'=32] {'sub'}, dimensions={1}, use_global_device_ids=true | all-gather | bytes 118272 | tf_op jit(solution)/shard_map/all_gather | solution.py:92
  505.0 2.2 fusion.23
  507.2 32.5 %all_gather.49 = f32[7,4096]{1,0:T(8,128)S(1)} all-gather(f32[7,128]{1,0:T(8,128)S(1)} %pad_maximum_fusion), channel_id=1, replica_groups=mesh['grp'=8,'sub'=32] {'sub'}, dimensions={1}, use_global_device_ids=true | all-gather | bytes 118272 | tf_op jit(solution)/shard_map/all_gather | solution.py:92
  542.4 2.2 fusion.25
  544.6 35.3 %all_gather.50 = f32[4,4096]{1,0:T(4,128)S(1)} all-gather(f32[4,128]{1,0:T(4,128)S(1)} %pad_maximum_fusion.9), channel_id=1, replica_groups=mesh['grp'=8,'sub'=32] {'sub'}, dimensions={1}, use_global_device_ids=true | all-gather | bytes 67584 | tf_op jit(solution)/shard_map/all_gather | solution.py:79
  579.9 10.4 %while.10 = (s32[]{:T(128)}, f32[4,3,1024]{2,1,0:T(4,128)S(1)}, f32[3,512]{1,0:T(4,128)S(1)}, f32[4,3,1024]{2,1,0:T(4,128)S(1)}, f32[512]{0:T(512)S(1)}, /*index=5*/s32[]{:T(128)}) while((s32[]{:T(128)}, f32[4,3,1024]{2,1,0:T(4,128)S(1)}, f32[3,512]{1,0:T(4,128)S(1)}, f32[4,3,1024]{2,1,0:T(4,128)S(1)}, f32[512]{0:T(512)S(1)}, ...), condition=%wide.region_49.50_spmd, body=%wide.region_46.49_spmd.sunk | while | flops 11006978 | bytes 8497229 | solution.py:34
  591.0 8.5 %while.11 = (s32[]{:T(128)}, f32[4,3,128]{2,1,0:T(4,128)S(1)}, f32[3,4096]{1,0:T(4,128)S(1)}, f32[4,3,128]{2,1,0:T(4,128)S(1)}, f32[1,4096]{1,0:T(1,128)S(1)}, /*index=5*/s32[]{:T(128)}) while((s32[]{:T(128)}, f32[4,3,128]{2,1,0:T(4,128)S(1)}, f32[3,4096]{1,0:T(4,128)S(1)}, f32[4,3,128]{2,1,0:T(4,128)S(1)}, f32[1,4096]{1,0:T(1,128)S(1)}, ...), condition=%wide.region_54.55_spmd, body=%wide.region_51.54_spmd.sunk | while | flops 11009666 | bytes 8515149 | solution.py:34
  600.1 211.7 %all-gather.5.cloned.1.call-done = f32[256,3,4096]{2,1,0:T(4,128)} async-done(((f32[1,3,4096]{2,1,0:T(4,128)}), f32[256,3,4096]{2,1,0:T(4,128)}) %all-gather.5.cloned.1.call-update) | async-done | bytes 12582928 | tf_op jit(solution)/shard_map/all_gather | solution.py:82
  811.8 8.8 %reduce_sum.497 = f32[3,4096]{1,0:T(4,128)S(1)} reduce(f32[256,3,4096]{2,1,0:T(4,128)} %all-gather.5.cloned.1.call-done, f32[]{:T(128)} %constant.221.clone.1), dimensions={0}, to_apply=%region_50.51 | reduce | flops 3133440 | bytes 12632068 | tf_op jit(solution)/shard_map/reduce_sum | solution.py:83
  (174 shorter events, 65.1 us)
Async XLA Ops:
  7.2 193.9 %all-gather.3.cloned.1.call-start = ((), (), s32[]{:S(2)}) async-start(), calls=%async_computation | async-start | bytes 16842752 | tf_op jit(solution)/shard_map/all_gather | solution.py:82
  51.5 0.7 copy-start
  55.1 0.7 copy-start
  58.7 0.7 copy-start
  62.4 0.7 copy-start
  64.3 0.6 copy-start.2
  65.0 746.8 %all-gather.5.cloned.1.call-start = ((), (), s32[]{:S(2)}) async-start(), calls=%async_computation.1 | async-start | bytes 16842752 | tf_op jit(solution)/shard_map/all_gather | solution.py:82
  65.1 11.2 %copy-start.5 = (f32[3,512]{1,0:T(4,128)S(1)}, f32[3,512]{1,0:T(4,128)}, u32[]{:S(2)}) copy-start(f32[3,512]{1,0:T(4,128)} %param.19) | copy-start | bytes 18436
  77.0 132.9 %copy-start.7 = (f32[3,128]{1,0:T(4,128)S(1)}, f32[3,128]{1,0:T(4,128)}, u32[]{:S(2)}) copy-start(f32[3,128]{1,0:T(4,128)} %param.16) | copy-start | bytes 4612
  77.0 132.9 %copy-start.4 = (f32[3,128]{1,0:T(4,128)S(1)}, f32[3,128]{1,0:T(4,128)}, u32[]{:S(2)}) copy-start(f32[3,128]{1,0:T(4,128)} %param.15) | copy-start | bytes 4612
  544.6 35.3 %copy-start.6 = (f32[3,128]{1,0:T(4,128)}, f32[3,128]{1,0:T(4,128)S(1)}, u32[]{:S(2)}) copy-start(f32[3,128]{1,0:T(4,128)S(1)} %multiply_add_fusion.2) | copy-start | bytes 4612
  590.3 0.6 copy-start.3
  599.5 221.1 %copy-start.1 = (f32[4,3,128]{2,1,0:T(4,128)}, f32[4,3,128]{2,1,0:T(4,128)S(1)}, u32[]{:S(2)}) copy-start(f32[4,3,128]{2,1,0:T(4,128)S(1)} %get-tuple-element.614) | copy-start | bytes 18436
Sparse Core Ops, SparseCore 0:
  65.1 135.9 all-gather.2
  591.1 220.6 all-gather.4
